TPU v7x, 32 devices: a whole 2x2x4 slice. The times are simulated.
32 devices in a mesh: ctx: 8 (over z, y), fsdp: 4 (over x, core).
Axes of the slice: x: 2, y: 2, z: 4, core: 2. Of those that a mesh axis runs over, the one named last changes fastest.
Arguments:
- tokens: bfloat16 [4, 4096, 1024], P('fsdp', 'ctx'), may hold values from -6 to 6
- block_pos: int32 [4, 16], P('fsdp'), may hold values from 0 to 15, each once within a row
- gain_attn: bfloat16 [1024], P('fsdp'), may hold values from 0.25 to 1.75
- w_query: bfloat16 [1024, 256], P('fsdp'), may hold values from -0.1875 to 0.1875
- w_key: bfloat16 [1024, 256], P('fsdp'), may hold values from -0.1875 to 0.1875
- w_value: bfloat16 [1024, 1024], P('fsdp'), may hold values from -0.1875 to 0.1875
- w_out: bfloat16 [1024, 1024], P('fsdp'), may hold values from -2 to 2
- gain_ffn: bfloat16 [1024], P('fsdp'), may hold values from 0.25 to 1.75
- w_gate: bfloat16 [1024, 2752], P('fsdp'), may hold values from -0.1875 to 0.1875
- w_up: bfloat16 [1024, 2752], P('fsdp'), may hold values from -0.1875 to 0.1875
- w_down: bfloat16 [2752, 1024], P('fsdp'), may hold values from -0.109375 to 0.109375
- cotangent: bfloat16 [4, 4096, 1024], P('fsdp', 'ctx'), may hold values from -6 to 6
Outputs:
- output: bfloat16 [4, 4096, 1024], P('fsdp', 'ctx')
- grad_tokens: float32 [4, 4096, 1024], P('fsdp', 'ctx')
- grad_gain_attn: float32 [1024], P('fsdp')
- grad_query: float32 [1024, 256], P('fsdp')
- grad_key: float32 [1024, 256], P('fsdp')
- grad_value: float32 [1024, 1024], P('fsdp')
- grad_out: float32 [1024, 1024], P('fsdp')
- grad_gain_ffn: float32 [1024], P('fsdp')
- grad_gate: float32 [1024, 2752], P('fsdp')
- grad_up: float32 [1024, 2752], P('fsdp')
- grad_down: float32 [2752, 1024], P('fsdp')
Inputs may be any that keep to these rules, and one draw needn't show every extreme that they name: `block_pos`: each row is a permutation of the 16 position blocks of one sequence.
All inputs are finite; a program needn't handle non-finite values.
Results may differ from a plain program's by a relative error of at most 0.015.
Values may be sent and summed in bfloat16 or wider, within the bound.
A program may use at most 512 MiB of HBM per device.

v0:
```python
import jax
import jax.numpy as jnp
from jax import lax
from jax.sharding import PartitionSpec as P

HEADS = 16
FDIM = 16
VDIM = 64
BLOCK = 256
highest = lax.Precision.HIGHEST
eps_norm = 1e-05
root_half = 0.7071067811865476


def features(scaled):
    outer_prod = scaled[..., :, None] * scaled[..., None, :]
    flattened = (
        outer_prod.reshape(scaled.shape[:-1] + (scaled.shape[-1] * scaled.shape[-1],)) * root_half
    )
    constant = jnp.ones(scaled.shape[:-1] + (1,), jnp.float32)
    return jnp.concatenate([constant, scaled, flattened], axis=-1)


def features_back(scaled, grad_feat):
    feat_dim = scaled.shape[-1]
    linear = grad_feat[..., 1 : 1 + feat_dim]
    square = (
        grad_feat[..., 1 + feat_dim :].reshape(scaled.shape[:-1] + (feat_dim, feat_dim)) * root_half
    )
    return linear + jnp.einsum("...ab,...b->...a", square + jnp.swapaxes(square, -1, -2), scaled)


def norm_forward(values, gain_vector):
    inv_rms = lax.rsqrt(jnp.mean(values * values, axis=-1, keepdims=True) + eps_norm)
    return (values * inv_rms * gain_vector, inv_rms)


def norm_backward(values, inv_rms, gain_vector, grad_normed):
    weighted = grad_normed * gain_vector
    grad_gain = jnp.sum(grad_normed * values * inv_rms, axis=0)
    grad_values = inv_rms * weighted - values * (inv_rms * inv_rms * inv_rms) * jnp.mean(
        weighted * values, axis=-1, keepdims=True
    )
    return (grad_values, grad_gain)


def block_group():
    for group_size in (8, 4, 2):
        return group_size
    return 1


def body(
    tokens,
    block_pos,
    gain_attn,
    w_query,
    w_key,
    w_value,
    w_out,
    gain_ffn,
    w_gate,
    w_up,
    w_down,
    cotangent,
):
    gathered = (
        lax.all_gather(gain_attn, "fsdp", axis=0, tiled=True),
        lax.all_gather(w_query, "fsdp", axis=0, tiled=True),
        lax.all_gather(w_key, "fsdp", axis=0, tiled=True),
        lax.all_gather(w_value, "fsdp", axis=0, tiled=True),
        lax.all_gather(w_out, "fsdp", axis=0, tiled=True),
        lax.all_gather(gain_ffn, "fsdp", axis=0, tiled=True),
        lax.all_gather(w_gate, "fsdp", axis=0, tiled=True),
        lax.all_gather(w_up, "fsdp", axis=0, tiled=True),
        lax.all_gather(w_down, "fsdp", axis=0, tiled=True),
    )
    norm_one_gain = gathered[0].astype(jnp.float32)
    query_full, key_full, value_full, out_full = (
        gathered[1],
        gathered[2],
        gathered[3],
        gathered[4],
    )
    norm_two_gain = gathered[5].astype(jnp.float32)
    gate_full, up_full, down_full = (gathered[6], gathered[7], gathered[8])
    residual = tokens[0].astype(jnp.float32)
    row_count = residual.shape[0]
    local_blocks = row_count // BLOCK
    feat_width = 1 + FDIM + FDIM * FDIM
    positions = block_pos[0]
    own_positions = lax.dynamic_slice_in_dim(
        positions, lax.axis_index("ctx") * local_blocks, local_blocks
    )
    normed_one, inv_rms_one = norm_forward(residual, norm_one_gain)
    normed_one_low = normed_one.astype(jnp.bfloat16)
    queries = jnp.dot(normed_one_low, query_full, preferred_element_type=jnp.float32).astype(
        jnp.bfloat16
    )
    keys_all = jnp.dot(normed_one_low, key_full, preferred_element_type=jnp.float32).astype(
        jnp.bfloat16
    )
    values_all = jnp.dot(normed_one_low, value_full, preferred_element_type=jnp.float32).astype(
        jnp.bfloat16
    )
    query_blocks = queries.reshape(local_blocks, BLOCK, HEADS, FDIM)
    key_blocks = keys_all.reshape(local_blocks, BLOCK, HEADS, FDIM)
    value_blocks = values_all.reshape(local_blocks, BLOCK, HEADS, VDIM)
    query_scaled = query_blocks.astype(jnp.float32) * 0.5
    key_scaled = key_blocks.astype(jnp.float32) * 0.5
    phi_query = features(query_scaled).astype(jnp.bfloat16)
    phi_key = features(key_scaled).astype(jnp.bfloat16)
    state_zero = jnp.zeros((local_blocks, HEADS, feat_width, VDIM), jnp.float32)
    norm_zero = jnp.zeros((local_blocks, HEADS, feat_width), jnp.float32)
    running = (state_zero, norm_zero)
    key_piece = lax.all_gather(keys_all, "ctx", axis=0, tiled=True)
    value_piece = lax.all_gather(values_all, "ctx", axis=0, tiled=True)
    block_count = key_piece.shape[0] // BLOCK
    group_size = block_group()
    others = positions
    key_groups = key_piece.reshape(block_count // group_size, group_size, BLOCK, HEADS, FDIM)
    value_groups = value_piece.reshape(block_count // group_size, group_size, BLOCK, HEADS, VDIM)
    other_groups = others.reshape(block_count // group_size, group_size)

    def one_group(inner_sum, group_args):
        keys_here, values_here, places = group_args
        key_feat = features(keys_here.astype(jnp.float32) * 0.5).astype(jnp.bfloat16)
        states = jnp.einsum(
            "gthf,gthv->ghfv", key_feat, values_here, preferred_element_type=jnp.float32
        )
        norm_sums = jnp.sum(key_feat.astype(jnp.float32), axis=1)
        earlier = (places[None, :] < own_positions[:, None]).astype(jnp.float32)
        return (
            (
                inner_sum[0] + jnp.einsum("ig,ghfv->ihfv", earlier, states, precision=highest),
                inner_sum[1] + jnp.einsum("ig,ghf->ihf", earlier, norm_sums, precision=highest),
            ),
            None,
        )

    running, unused = lax.scan(one_group, running, (key_groups, value_groups, other_groups))
    prefix, prefix_norm = running
    phi_query_wide = phi_query.astype(jnp.float32)
    scores = (
        jnp.einsum("nshf,nthf->nhst", query_blocks, key_blocks, preferred_element_type=jnp.float32)
        * 0.25
    )
    kernel = 1.0 + scores + 0.5 * scores * scores
    kernel_low = kernel.astype(jnp.bfloat16)
    numerator = jnp.einsum(
        "nhst,nthv->nshv", kernel_low, value_blocks, preferred_element_type=jnp.float32
    ) + jnp.einsum("nshf,nhfv->nshv", phi_query_wide, prefix, precision=highest)
    denominator = jnp.transpose(jnp.sum(kernel, axis=-1), (0, 2, 1)) + jnp.einsum(
        "nshf,nhf->nsh", phi_query_wide, prefix_norm, precision=highest
    )
    attention_full = numerator / denominator[..., None]
    attention_low = attention_full.reshape(row_count, HEADS * VDIM).astype(jnp.bfloat16)
    middle = residual + jnp.dot(attention_low, out_full, preferred_element_type=jnp.float32)
    normed_two, inv_rms_two = norm_forward(middle, norm_two_gain)
    normed_two_low = normed_two.astype(jnp.bfloat16)
    gate_pre = jnp.dot(normed_two_low, gate_full, preferred_element_type=jnp.float32)
    up_pre = jnp.dot(normed_two_low, up_full, preferred_element_type=jnp.float32)
    sigmoid_gate = jax.nn.sigmoid(gate_pre)
    silu_gate = gate_pre * sigmoid_gate
    hidden_low = (silu_gate * up_pre).astype(jnp.bfloat16)
    result = middle + jnp.dot(hidden_low, down_full, preferred_element_type=jnp.float32)
    output = result.astype(jnp.bfloat16)[None]
    cotangent_low = cotangent[0]
    grad_out_full = cotangent_low.astype(jnp.float32)
    grad_down_full = jnp.einsum(
        "tf,td->fd", hidden_low, cotangent_low, preferred_element_type=jnp.float32
    )
    grad_hidden = jnp.einsum(
        "td,fd->tf", cotangent_low, down_full, preferred_element_type=jnp.float32
    )
    grad_gate_pre = (
        grad_hidden * up_pre * (sigmoid_gate * (1.0 + gate_pre * (1.0 - sigmoid_gate)))
    ).astype(jnp.bfloat16)
    grad_up_pre = (grad_hidden * silu_gate).astype(jnp.bfloat16)
    grad_gate_full = jnp.einsum(
        "td,tf->df", normed_two_low, grad_gate_pre, preferred_element_type=jnp.float32
    )
    grad_up_full = jnp.einsum(
        "td,tf->df", normed_two_low, grad_up_pre, preferred_element_type=jnp.float32
    )
    grad_normed_two = jnp.einsum(
        "tf,df->td", grad_gate_pre, gate_full, preferred_element_type=jnp.float32
    ) + jnp.einsum("tf,df->td", grad_up_pre, up_full, preferred_element_type=jnp.float32)
    grad_middle_norm, grad_gain_two = norm_backward(
        middle, inv_rms_two, norm_two_gain, grad_normed_two
    )
    grad_middle = grad_out_full + grad_middle_norm
    grad_branch = grad_middle.astype(jnp.bfloat16)
    grad_out_proj = jnp.einsum(
        "ta,td->ad", attention_low, grad_branch, preferred_element_type=jnp.float32
    )
    grad_attention = jnp.einsum(
        "td,ad->ta", grad_branch, out_full, preferred_element_type=jnp.float32
    )
    grad_attention = grad_attention.reshape(local_blocks, BLOCK, HEADS, VDIM)
    grad_numerator = (grad_attention / denominator[..., None]).astype(jnp.bfloat16)
    grad_denominator = (-jnp.sum(grad_attention * attention_full, axis=-1) / denominator).astype(
        jnp.bfloat16
    )
    grad_denom_wide = grad_denominator.astype(jnp.float32)
    grad_kernel = (
        jnp.einsum(
            "nshv,nthv->nhst", grad_numerator, value_blocks, preferred_element_type=jnp.float32
        )
        + jnp.transpose(grad_denom_wide, (0, 2, 1))[..., None]
    )
    grad_scores = ((1.0 + scores) * grad_kernel).astype(jnp.bfloat16)
    flat_numer = grad_numerator.reshape(row_count, HEADS * VDIM)
    flat_denom = grad_denominator.reshape(row_count, HEADS)
    running = (state_zero, norm_zero)
    query_piece = lax.all_gather(queries, "ctx", axis=0, tiled=True)
    numer_piece = lax.all_gather(flat_numer, "ctx", axis=0, tiled=True)
    denom_piece = lax.all_gather(flat_denom, "ctx", axis=0, tiled=True)
    block_count = query_piece.shape[0] // BLOCK
    group_size = block_group()
    others = positions
    query_groups = query_piece.reshape(block_count // group_size, group_size, BLOCK, HEADS, FDIM)
    numer_groups = numer_piece.reshape(block_count // group_size, group_size, BLOCK, HEADS, VDIM)
    denom_groups = denom_piece.reshape(block_count // group_size, group_size, BLOCK, HEADS)
    other_groups = others.reshape(block_count // group_size, group_size)

    def one_group(inner_sum, group_args):
        queries_here, numer_here, denom_here, places = group_args
        query_feat = features(queries_here.astype(jnp.float32) * 0.5).astype(jnp.bfloat16)
        grad_states = jnp.einsum(
            "gthf,gthv->ghfv", query_feat, numer_here, preferred_element_type=jnp.float32
        )
        grad_norms = jnp.einsum(
            "gthf,gth->ghf", query_feat, denom_here, preferred_element_type=jnp.float32
        )
        later_mask = (places[None, :] > own_positions[:, None]).astype(jnp.float32)
        return (
            (
                inner_sum[0]
                + jnp.einsum("ig,ghfv->ihfv", later_mask, grad_states, precision=highest),
                inner_sum[1] + jnp.einsum("ig,ghf->ihf", later_mask, grad_norms, precision=highest),
            ),
            None,
        )

    running, unused = lax.scan(
        one_group, running, (query_groups, numer_groups, denom_groups, other_groups)
    )
    later_states, later_norms = running
    grad_phi_query = (
        jnp.einsum("nshv,nhfv->nshf", grad_numerator.astype(jnp.float32), prefix, precision=highest)
        + grad_denom_wide[..., None] * prefix_norm[:, None, :, :]
    )
    grad_phi_key = (
        jnp.einsum(
            "nthv,nhfv->nthf", value_blocks.astype(jnp.float32), later_states, precision=highest
        )
        + later_norms[:, None, :, :]
    )
    grad_values = jnp.einsum(
        "nhst,nshv->nthv", kernel_low, grad_numerator, preferred_element_type=jnp.float32
    ) + jnp.einsum("nthf,nhfv->nthv", phi_key.astype(jnp.float32), later_states, precision=highest)
    grad_values_low = grad_values.reshape(row_count, HEADS * VDIM).astype(jnp.bfloat16)
    grad_queries = jnp.einsum(
        "nhst,nthf->nshf", grad_scores, key_blocks, preferred_element_type=jnp.float32
    ) * 0.25 + 0.5 * features_back(query_scaled, grad_phi_query)
    grad_queries_low = grad_queries.reshape(row_count, HEADS * FDIM).astype(jnp.bfloat16)
    grad_keys = jnp.einsum(
        "nhst,nshf->nthf", grad_scores, query_blocks, preferred_element_type=jnp.float32
    ) * 0.25 + 0.5 * features_back(key_scaled, grad_phi_key)
    grad_keys_low = grad_keys.reshape(row_count, HEADS * FDIM).astype(jnp.bfloat16)
    grad_query_full = jnp.einsum(
        "td,tk->dk", normed_one_low, grad_queries_low, preferred_element_type=jnp.float32
    )
    grad_key_full = jnp.einsum(
        "td,tk->dk", normed_one_low, grad_keys_low, preferred_element_type=jnp.float32
    )
    grad_value_full = jnp.einsum(
        "td,tk->dk", normed_one_low, grad_values_low, preferred_element_type=jnp.float32
    )
    grad_normed_one = (
        jnp.einsum("tk,dk->td", grad_queries_low, query_full, preferred_element_type=jnp.float32)
        + jnp.einsum("tk,dk->td", grad_keys_low, key_full, preferred_element_type=jnp.float32)
        + jnp.einsum("tk,dk->td", grad_values_low, value_full, preferred_element_type=jnp.float32)
    )
    grad_from_norm, grad_gain_one = norm_backward(
        residual, inv_rms_one, norm_one_gain, grad_normed_one
    )
    grad_tokens = (grad_middle + grad_from_norm)[None]
    shards = (
        lax.psum_scatter(
            grad_gain_one.astype(jnp.bfloat16), "fsdp", scatter_dimension=0, tiled=True
        ).astype(jnp.float32),
        lax.psum_scatter(
            grad_query_full.astype(jnp.bfloat16), "fsdp", scatter_dimension=0, tiled=True
        ).astype(jnp.float32),
        lax.psum_scatter(
            grad_key_full.astype(jnp.bfloat16), "fsdp", scatter_dimension=0, tiled=True
        ).astype(jnp.float32),
        lax.psum_scatter(
            grad_value_full.astype(jnp.bfloat16), "fsdp", scatter_dimension=0, tiled=True
        ).astype(jnp.float32),
        lax.psum_scatter(
            grad_out_proj.astype(jnp.bfloat16), "fsdp", scatter_dimension=0, tiled=True
        ).astype(jnp.float32),
        lax.psum_scatter(
            grad_gain_two.astype(jnp.bfloat16), "fsdp", scatter_dimension=0, tiled=True
        ).astype(jnp.float32),
        lax.psum_scatter(
            grad_gate_full.astype(jnp.bfloat16), "fsdp", scatter_dimension=0, tiled=True
        ).astype(jnp.float32),
        lax.psum_scatter(
            grad_up_full.astype(jnp.bfloat16), "fsdp", scatter_dimension=0, tiled=True
        ).astype(jnp.float32),
        lax.psum_scatter(
            grad_down_full.astype(jnp.bfloat16), "fsdp", scatter_dimension=0, tiled=True
        ).astype(jnp.float32),
    )
    totals = lax.psum(
        (
            shards[0],
            shards[1],
            shards[2],
            shards[3],
            shards[4],
            shards[5],
            shards[6],
            shards[7],
            shards[8],
        ),
        "ctx",
    )
    return (
        output,
        grad_tokens,
        totals[0],
        totals[1],
        totals[2],
        totals[3],
        totals[4],
        totals[5],
        totals[6],
        totals[7],
        totals[8],
    )


def solution(mesh):
    in_specs = (
        P("fsdp", "ctx", None),
        P("fsdp", None),
        P("fsdp"),
        P("fsdp", None),
        P("fsdp", None),
        P("fsdp", None),
        P("fsdp", None),
        P("fsdp"),
        P("fsdp", None),
        P("fsdp", None),
        P("fsdp", None),
        P("fsdp", "ctx", None),
    )
    out_specs = (
        P("fsdp", "ctx", None),
        P("fsdp", "ctx", None),
        P("fsdp"),
        P("fsdp", None),
        P("fsdp", None),
        P("fsdp", None),
        P("fsdp", None),
        P("fsdp"),
        P("fsdp", None),
        P("fsdp", None),
        P("fsdp", None),
    )
    return jax.shard_map(body, mesh=mesh, in_specs=in_specs, out_specs=out_specs, check_vma=False)
```

profile of v0, /device:TPU:0, one launch (start us, length us, event | category | flops | bytes accessed | tf_op | source)
XLA Modules:
  0.0 1292.5 jit_solution(17293718670228395038)
XLA Ops:
  16.1 9.3 all_gather.45
  96.9 118.5 %all-gather.16.cloned.1.call-done = bf16[4096,1024]{1,0:T(8,128)(2,1)} async-done(((bf16[512,1024]{1,0:T(8,128)(2,1)}), bf16[4096,1024]{1,0:T(8,128)(2,1)}) %all-gather.16.cloned.1.call-update) | async-done | bytes 8388624 | tf_op jit(solution)/shard_map/all_gather | solution.py:117
  215.5 22.2 %reshape.269 = bf16[2,8,256,16,64]{4,3,2,1,0:T(8,128)(2,1)} reshape(bf16[4096,1024]{1,0:T(8,128)(2,1)} %all-gather.16.cloned.1.call-done) | data formatting | bytes 16777216 | tf_op jit(solution)/shard_map/reshape | solution.py:122
  237.7 19.7 %copy.112 = bf16[2,8,256,16,64]{2,4,3,1,0:T(8,128)(2,1)} copy(bf16[2,8,256,16,64]{4,3,2,1,0:T(8,128)(2,1)} %reshape.269) | data formatting | bytes 16777216
  257.4 111.2 %while.26 = (s32[]{:T(128)}, f32[2,16,273,64]{2,0,3,1:T(2,128)S(1)}, f32[2,16,273]{2,0,1:T(2,128)S(1)}, s32[2,8]{1,0:T(2,128)S(1)}, s32[2]{0:T(128)S(1)}, /*inde...) while((s32[]{:T(128)}, ...), condition=%wide.region_3.4_spmd.clone, body=%wide.region_1.3_spmd.clone.sunk | while | flops 1343690752 | bytes 159030480 | solution.py:141
  270.2 8.2 convert_reduce_fusion.2
  278.4 13.8 %fusion.184 = f32[8,16,273,64]{2,3,1,0:T(8,128)} fusion(bf16[8,256,16,256]{1,3,2,0:T(8,128)(2,1)} %bitcast.288, bf16[8,256,16,16]{1,3,2,0:T(8,128)(2,1)} %copy-done.1, bf16[273]{0:T(512)(128)(2,1)S(1)} %pad.clone.2, bf16[2,8,256,16,64]{2,4,3,1,0:T(8,128)(2,1)} %get-tuple-element.396, s32[]{:T(128)S(6)} %copy.272), kind=kOutput, calls=%fused_computation.5.clone.1 | convolution fusion | flops 1198718976 | bytes 30966310 | tf_op jit(solution)/shard_map/while/body/eval_jaxpr/gthf,gthv->ghfv/dot_general | solution.py:128
  292.3 19.9 %select_add_fusion.4 = f32[2,16,273,64]{2,0,3,1:T(2,128)S(1)} fusion(f32[2,16,273,64]{2,0,3,1:T(2,128)S(1)} %get-tuple-element.380, pred[]{:T(512)S(6)} %compare.6, f32[8,16,273,64]{2,3,1,0:T(8,128)} %fusion.184, s32[8]{0:T(128)S(1)} %fusion.185, s32[2]{0:T(128)S(1)} %get-tuple-element.394), kind=kOutput, calls=%fused_computation.9.clone.1 | convolution fusion | flops 54792208 | bytes 13418537 | tf_op jit(solution)/shard_map/while/body/eval_jaxpr/ig,ghfv->ihfv/dot_general | solution.py:135
  325.2 8.2 convert_reduce_fusion.2
  333.4 15.2 %fusion.184 = f32[8,16,273,64]{2,3,1,0:T(8,128)} fusion(bf16[8,256,16,256]{1,3,2,0:T(8,128)(2,1)} %bitcast.288, bf16[8,256,16,16]{1,3,2,0:T(8,128)(2,1)} %copy-done.1, bf16[273]{0:T(512)(128)(2,1)S(1)} %pad.clone.2, bf16[2,8,256,16,64]{2,4,3,1,0:T(8,128)(2,1)} %get-tuple-element.396, s32[]{:T(128)S(6)} %copy.272), kind=kOutput, calls=%fused_computation.5.clone.1 | convolution fusion | flops 1198718976 | bytes 30966310 | tf_op jit(solution)/shard_map/while/body/eval_jaxpr/gthf,gthv->ghfv/dot_general | solution.py:128
  348.6 19.3 %select_add_fusion.4 = f32[2,16,273,64]{2,0,3,1:T(2,128)S(1)} fusion(f32[2,16,273,64]{2,0,3,1:T(2,128)S(1)} %get-tuple-element.380, pred[]{:T(512)S(6)} %compare.6, f32[8,16,273,64]{2,3,1,0:T(8,128)} %fusion.184, s32[8]{0:T(128)S(1)} %fusion.185, s32[2]{0:T(128)S(1)} %get-tuple-element.394), kind=kOutput, calls=%fused_computation.9.clone.1 | convolution fusion | flops 54792208 | bytes 13418537 | tf_op jit(solution)/shard_map/while/body/eval_jaxpr/ig,ghfv->ihfv/dot_general | solution.py:135
  389.7 8.5 fusion.122
  398.3 8.7 fusion.121
  407.0 12.3 multiply_convert_fusion.5
  470.3 16.5 %fusion.44 = f32[2,256,16,16]{1,3,2,0:T(8,128)S(1)} fusion(f32[2,256,16,16,16]{1,4,3,2,0:T(8,128)} %bitcast.293, f32[2,256,16,16]{1,3,2,0:T(8,128)S(1)} %copy-done.21), kind=kLoop, calls=%fused_computation.67 | loop fusion | flops 6160384 | bytes 9437184 | tf_op jit(solution)/shard_map/...ab,...b->...a/dot_general | solution.py:30
  530.6 31.4 %all_gather.55 = bf16[4096,16]{0,1:T(8,128)(2,1)S(1)} all-gather(bf16[512,16]{0,1:T(8,128)(2,1)S(1)} %bitcast.321), channel_id=1, replica_groups=mesh['ctx'=8,'fsdp'=4] {'ctx'}, dimensions={0}, use_global_device_ids=true | all-gather | bytes 147456 | tf_op jit(solution)/shard_map/all_gather | solution.py:218
  569.9 22.2 %reshape.271 = bf16[2,8,256,16,64]{4,3,2,1,0:T(8,128)(2,1)} reshape(bf16[4096,1024]{1,0:T(8,128)(2,1)} %all-gather.28.cloned.1.call-done) | data formatting | bytes 16777216 | tf_op jit(solution)/shard_map/reshape | solution.py:223
  592.1 19.7 %copy.135 = bf16[2,8,256,16,64]{2,4,3,1,0:T(8,128)(2,1)} copy(bf16[2,8,256,16,64]{4,3,2,1,0:T(8,128)(2,1)} %reshape.271) | data formatting | bytes 16777216
  611.7 114.5 %while.27 = (s32[]{:T(128)}, f32[2,16,273,64]{2,0,3,1:T(2,128)S(1)}, f32[2,16,273]{2,0,1:T(2,128)S(1)}, s32[2,8]{1,0:T(2,128)S(1)}, s32[2]{0:T(128)S(1)}, /*inde...) while((s32[]{:T(128)}, ...), condition=%wide.region_9.10_spmd.clone, body=%wide.region_8.9_spmd.clone.sunk | while | flops 1352671360 | bytes 92249264 | solution.py:246
  614.5 8.8 multiply_convert_fusion.12
  623.3 9.2 fusion.193
  632.5 16.2 %fusion.191 = f32[8,16,273,64]{2,3,1,0:T(8,128)} fusion(bf16[8,256,16,256]{1,3,2,0:T(8,128)(2,1)} %bitcast.290, bf16[8,256,16,16]{1,3,2,0:T(8,128)(2,1)} %copy-done.9, bf16[273]{0:T(512)(128)(2,1)S(1)} %pad.3.clone.2, bf16[2,8,256,16,64]{2,4,3,1,0:T(8,128)(2,1)} %get-tuple-element.431, s32[]{:T(128)S(6)} %copy.281), kind=kOutput, calls=%fused_computation.30.clone.1 | convolution fusion | flops 1198718976 | bytes 30966310 | tf_op jit(solution)/shard_map/while/body/eval_jaxpr/gthf,gthv->ghfv/dot_general | solution.py:230
  648.8 19.8 %select_add_fusion.5 = f32[2,16,273,64]{2,0,3,1:T(2,128)S(1)} fusion(f32[2,16,273,64]{2,0,3,1:T(2,128)S(1)} %get-tuple-element.414, pred[]{:T(512)S(6)} %compare.7, f32[8,16,273,64]{2,3,1,0:T(8,128)} %fusion.191, s32[8]{0:T(128)S(1)} %fusion.192, s32[2]{0:T(128)S(1)} %get-tuple-element.429), kind=kOutput, calls=%fused_computation.35.clone.1 | convolution fusion | flops 54792208 | bytes 13418537 | tf_op jit(solution)/shard_map/while/body/eval_jaxpr/ig,ghfv->ihfv/dot_general | solution.py:240
  671.6 8.8 multiply_convert_fusion.12
  680.4 9.3 fusion.193
  689.7 16.1 %fusion.191 = f32[8,16,273,64]{2,3,1,0:T(8,128)} fusion(bf16[8,256,16,256]{1,3,2,0:T(8,128)(2,1)} %bitcast.290, bf16[8,256,16,16]{1,3,2,0:T(8,128)(2,1)} %copy-done.9, bf16[273]{0:T(512)(128)(2,1)S(1)} %pad.3.clone.2, bf16[2,8,256,16,64]{2,4,3,1,0:T(8,128)(2,1)} %get-tuple-element.431, s32[]{:T(128)S(6)} %copy.281), kind=kOutput, calls=%fused_computation.30.clone.1 | convolution fusion | flops 1198718976 | bytes 30966310 | tf_op jit(solution)/shard_map/while/body/eval_jaxpr/gthf,gthv->ghfv/dot_general | solution.py:230
  705.7 19.7 %select_add_fusion.5 = f32[2,16,273,64]{2,0,3,1:T(2,128)S(1)} fusion(f32[2,16,273,64]{2,0,3,1:T(2,128)S(1)} %get-tuple-element.414, pred[]{:T(512)S(6)} %compare.7, f32[8,16,273,64]{2,3,1,0:T(8,128)} %fusion.191, s32[8]{0:T(128)S(1)} %fusion.192, s32[2]{0:T(128)S(1)} %get-tuple-element.429), kind=kOutput, calls=%fused_computation.35.clone.1 | convolution fusion | flops 54792208 | bytes 13418537 | tf_op jit(solution)/shard_map/while/body/eval_jaxpr/ig,ghfv->ihfv/dot_general | solution.py:240
  739.2 17.3 %fusion.41 = f32[2,256,16,16]{1,3,2,0:T(8,128)} fusion(f32[2,256,16,16,16]{1,4,3,2,0:T(8,128)} %bitcast.294, f32[2,256,16,16]{1,3,2,0:T(8,128)S(1)} %copy-done.23), kind=kLoop, calls=%fused_computation.63 | loop fusion | flops 6160384 | bytes 9437184 | tf_op jit(solution)/shard_map/...ab,...b->...a/dot_general | solution.py:30
  761.8 8.4 fusion.48
  813.0 7.9 reduce-scatter.10.cloned.1.call-done
  820.9 34.4 %reduce-scatter.12.cloned.1.call-done = bf16[256,1024]{1,0:T(8,128)(2,1)} async-done(((bf16[1024,1024]{1,0:T(8,128)(2,1)}), bf16[256,1024]{1,0:T(8,128)(2,1)}) %reduce-scatter.12.cloned.1.call-update) | async-done | bytes 524304 | tf_op jit(solution)/shard_map/reduce_scatter | solution.py:300
  855.3 430.5 %all-reduce.5 = (f32[256]{0:T(256)}, f32[256,256]{1,0:T(8,128)}, f32[256,256]{1,0:T(8,128)}, f32[256,1024]{1,0:T(8,128)}, f32[256,1024]{1,0:T(8,128)}, /*index=5...) all-reduce(f32[256]{0:T(256)S(1)} %get-tuple-element.267, ...), channel_id=1, replica_groups=mesh['ctx'=8,'fsdp'=4] {'ctx'}, use_global_device_ids=true, to_apply=%region_13.14 | all-reduce | flops 2769408 | bytes 16617472 | tf_op jit(solution)/shard_map/psum | solution.py:319
  (318 shorter events, 295.4 us)
Async XLA Ops:
  7.2 28.8 %copy-start.11 = (bf16[1,512,1024]{2,1,0:T(8,128)(2,1)S(1)}, bf16[1,512,1024]{2,1,0:T(8,128)(2,1)}, u32[]{:S(2)}) copy-start(bf16[1,512,1024]{2,1,0:T(8,128)(2,1)} %param.16) | copy-start | bytes 3145732
  7.2 28.7 %all-gather.12.cloned.1.call-start = ((), (), s32[]{:S(2)}) async-start(), calls=%async_computation.7 | async-start | bytes 2621440 | tf_op jit(solution)/shard_map/all_gather | solution.py:71
  7.9 81.4 %all-gather.14.cloned.1.call-start = ((), (), s32[]{:S(2)}) async-start(), calls=%async_computation.8 | async-start | bytes 2359296 | tf_op jit(solution)/shard_map/all_gather | solution.py:116
  14.6 35.1 %copy-start.53 = (f32[4,1,256]{2,1,0:T(1,128)}, f32[4,1,256]{2,1,0:T(1,128)S(1)}, u32[]{:S(2)}) copy-start(f32[4,1,256]{2,1,0:T(1,128)S(1)} %convert_element_type.281) | copy-start | bytes 12292
  26.1 23.6 %copy-start.58 = (f32[512]{0:T(512)}, f32[512]{0:T(512)S(1)}, u32[]{:S(2)}) copy-start(f32[512]{0:T(512)S(1)} %get-tuple-element.253) | copy-start | bytes 6148
  28.7 186.7 %all-gather.16.cloned.1.call-start = ((), (), s32[]{:S(2)}) async-start(), calls=%async_computation.9 | async-start | bytes 9437184 | tf_op jit(solution)/shard_map/all_gather | solution.py:117
  39.8 343.9 %all-gather.18.cloned.1.call-start = ((), (), s32[]{:S(2)}) async-start(), calls=%async_computation.10 | async-start | bytes 2621440 | tf_op jit(solution)/shard_map/all_gather | solution.py:72
  40.4 13.2 %copy-start.39 = (bf16[512,256]{1,0:T(8,128)(2,1)S(1)}, bf16[512,256]{1,0:T(8,128)(2,1)}, u32[]{:S(2)}) copy-start(bf16[512,256]{1,0:T(8,128)(2,1)} %convolution_convert_fusion.8) | copy-start | bytes 786436
  40.4 349.3 %all-gather.22.cloned.1.call-start = ((), (), s32[]{:S(2)}) async-start(), calls=%async_computation.12 | async-start | bytes 7045120 | tf_op jit(solution)/shard_map/all_gather | solution.py:75
  41.0 13.4 %copy-start.66 = (s32[1,16]{1,0:T(1,128)S(1)}, s32[1,16]{1,0:T(1,128)}, u32[]{:S(2)}) copy-start(s32[1,16]{1,0:T(1,128)} %param.17) | copy-start | bytes 196
  41.0 14.7 %copy-start.67 = (bf16[256]{0:T(256)(128)(2,1)S(1)}, bf16[256]{0:T(256)(128)(2,1)}, u32[]{:S(2)}) copy-start(bf16[256]{0:T(256)(128)(2,1)} %param.23) | copy-start | bytes 1540
  41.0 357.3 %all-gather.20.cloned.1.call-start = ((), (), s32[]{:S(2)}) async-start(), calls=%async_computation.11 | async-start | bytes 7045120 | tf_op jit(solution)/shard_map/all_gather | solution.py:74
  41.6 365.4 %all-gather.24.cloned.1.call-start = ((), (), s32[]{:S(2)}) async-start(), calls=%async_computation.13 | async-start | bytes 7045120 | tf_op jit(solution)/shard_map/all_gather | solution.py:76
  42.3 480.5 %all-gather.26.cloned.1.call-start = ((), (), s32[]{:S(2)}) async-start(), calls=%async_computation.14 | async-start | bytes 2359296 | tf_op jit(solution)/shard_map/all_gather | solution.py:216
  51.7 518.2 %all-gather.28.cloned.1.call-start = ((), (), s32[]{:S(2)}) async-start(), calls=%async_computation.15 | async-start | bytes 9437184 | tf_op jit(solution)/shard_map/all_gather | solution.py:217
  257.3 111.2 %copy-start.64 = (bf16[273]{0:T(512)(128)(2,1)S(1)}, bf16[273]{0:T(512)(128)(2,1)}, u32[]{:S(2)}) copy-start(bf16[273]{0:T(512)(128)(2,1)} %pad.9.clone) | copy-start | bytes 1642
  444.8 348.6 %reduce-scatter.8.cloned.1.call-start = ((), (), s32[]{:S(2)}) async-start(), calls=%async_computation.16 | async-start | bytes 655360 | tf_op jit(solution)/shard_map/reduce_scatter | solution.py:294
  457.1 29.7 %copy-start.10 = (bf16[2,256,16,64]{1,3,2,0:T(8,128)(2,1)}, bf16[2,256,16,64]{1,3,2,0:T(8,128)(2,1)S(1)}, u32[]{:S(2)}) copy-start(bf16[2,256,16,64]{1,3,2,0:T(8,128)(2,1)S(1)} %get-tuple-element.246) | copy-start | bytes 3145732
  470.3 16.5 %copy-start.16 = (bf16[2,256,16,64]{1,3,2,0:T(8,128)(2,1)S(1)}, bf16[2,256,16,64]{1,3,2,0:T(8,128)(2,1)}, u32[]{:S(2)}) copy-start(bf16[2,256,16,64]{1,3,2,0:T(8,128)(2,1)} %copy.107) | copy-start | bytes 3145732
  499.4 294.0 %reduce-scatter.14.cloned.1.call-start = ((), (), s32[]{:S(2)}) async-start(), calls=%async_computation.19 | async-start | bytes 2621440 | tf_op jit(solution)/shard_map/reduce_scatter | solution.py:303
  502.1 291.3 %reduce-scatter.20.cloned.1.call-start = ((), (), s32[]{:S(2)}) async-start(), calls=%async_computation.22 | async-start | bytes 7045120 | tf_op jit(solution)/shard_map/reduce_scatter | solution.py:315
  509.7 283.7 %reduce-scatter.18.cloned.1.call-start = ((), (), s32[]{:S(2)}) async-start(), calls=%async_computation.21 | async-start | bytes 7045120 | tf_op jit(solution)/shard_map/reduce_scatter | solution.py:312
  517.7 278.4 %reduce-scatter.16.cloned.1.call-start = ((), (), s32[]{:S(2)}) async-start(), calls=%async_computation.20 | async-start | bytes 7045120 | tf_op jit(solution)/shard_map/reduce_scatter | solution.py:309
  526.9 35.8 %copy-start.37 = (bf16[512,1024]{1,0:T(8,128)(2,1)S(1)}, bf16[512,1024]{1,0:T(8,128)(2,1)}, u32[]{:S(2)}) copy-start(bf16[512,1024]{1,0:T(8,128)(2,1)} %multiply_convert_fusion.8) | copy-start | bytes 3145732
  526.9 35.8 %copy-start.71 = (bf16[512,2752]{0,1:T(8,128)(2,1)S(1)}, bf16[512,2752]{0,1:T(8,128)(2,1)}, u32[]{:S(2)}) copy-start(bf16[512,2752]{0,1:T(8,128)(2,1)} %get-tuple-element.244) | copy-start | bytes 8454148
  567.6 253.3 %reduce-scatter.10.cloned.1.call-start = ((), (), s32[]{:S(2)}) async-start(), calls=%async_computation.17 | async-start | bytes 655360 | tf_op jit(solution)/shard_map/reduce_scatter | solution.py:297
  592.0 19.7 %copy-start.46 = (s32[2]{0:T(128)S(1)}, s32[2]{0:T(128)}, u32[]{:S(2)}) copy-start(s32[2]{0:T(128)} %copy-done.45) | copy-start | bytes 28
  592.0 19.7 %copy-start.69 = (s32[2,8]{1,0:T(2,128)S(1)}, s32[2,8]{1,0:T(2,128)}, u32[]{:S(2)}) copy-start(s32[2,8]{1,0:T(2,128)} %copy-done.68) | copy-start | bytes 196
  739.2 17.3 %copy-start.3 = (bf16[2,16,256,256]{2,3,1,0:T(8,128)(2,1)S(1)}, bf16[2,16,256,256]{2,3,1,0:T(8,128)(2,1)}, u32[]{:S(2)}) copy-start(bf16[2,16,256,256]{2,3,1,0:T(8,128)(2,1)} %copy-done.2) | copy-start | bytes 12582916
  739.2 17.3 %copy-start.29 = (bf16[2,256,16,16]{1,0,3,2:T(2,128)(2,1)S(1)}, bf16[2,256,16,16]{1,0,3,2:T(2,128)(2,1)}, u32[]{:S(2)}) copy-start(bf16[2,256,16,16]{1,0,3,2:T(2,128)(2,1)} %copy-done.28) | copy-start | bytes 786436
  770.2 85.1 %reduce-scatter.12.cloned.1.call-start = ((), (), s32[]{:S(2)}) async-start(), calls=%async_computation.18 | async-start | bytes 2621440 | tf_op jit(solution)/shard_map/reduce_scatter | solution.py:300
  803.5 51.8 %copy-start.48 = (bf16[256,256]{1,0:T(8,128)(2,1)S(1)}, bf16[256,256]{1,0:T(8,128)(2,1)}, u32[]{:S(2)}) copy-start(bf16[256,256]{1,0:T(8,128)(2,1)} %reduce-scatter.8.cloned.1.call-done) | copy-start | bytes 393220
  (61 other events, 305.2 us)
Sparse Core Ops, SparseCore 0:
  9.6 26.2 all-gather.11
  38.6 50.6 all-gather.13
  92.0 123.4 all-gather.15
  216.9 20.7 all-gather.17
  239.1 43.3 all-gather.21
  283.9 43.3 all-gather.19
  328.9 42.6 all-gather.23
  373.7 49.2 all-gather.25
  444.9 124.8 all-gather.27
  572.2 20.0 reduce-scatter.7
  594.9 31.4 reduce-scatter.13
  628.8 54.0 reduce-scatter.19
  685.6 53.9 reduce-scatter.17
  742.1 54.0 reduce-scatter.15
  799.2 21.6 reduce-scatter.9
  823.8 31.4 reduce-scatter.11
where the time goes:
time: 1300 us; the launch traced here: 1290 us
  blocking collectives  495 us (38%)
  matrix products  317 us (24%)
  waiting for transfers between devices  184 us (14%)
  local copies, waits for them, and re-layouts  168 us (13%)
  other arithmetic  111 us (9%)
  between operations  15.6 us (1%)
    psum x1, blocking collectives, body(): lax.psum((shards[0], shards[1], shards[2], shards[3], shards[4], shards[5...  430 us
    all_gather x1, waiting for transfers between devices, body(): value_piece = lax.all_gather(values_all, 'ctx', axis=0, tiled=True)  119 us
    unnamed x156, local copies, waits for them, and re-layouts  63.5 us
    dot_general x2, matrix products, one_group(): jnp.einsum('ig,ghfv->ihfv', later_mask, grad_states, precision=highest)  39.6 us
    dot_general x2, matrix products, one_group(): jnp.einsum('ig,ghfv->ihfv', earlier, states, precision=highest)  39.2 us
    another operation x12, other arithmetic  37.8 us
    reduce_scatter x1, waiting for transfers between devices, body(): lax.psum_scatter(grad_value_full.astype(jnp.bfloat16), 'fsdp', scatter_di...  34.4 us
    dot_general x2, other arithmetic, features_back(): jnp.einsum('...ab,...b->...a', square + jnp.swapaxes(square, -1, -2), sca...  33.7 us
  transfers between devices with their start and end apart: 16, of which 7 were waited for; matrix products, arithmetic and copies ran while one was open for 44% of the time, Pallas kernels for 0%

commit v1 on v0

--- a/solution.py
+++ b/solution.py
@@ -114,7 +114,9 @@
     norm_zero = jnp.zeros((local_blocks, HEADS, feat_width), jnp.float32)
     running = (state_zero, norm_zero)
     key_piece = lax.all_gather(keys_all, "ctx", axis=0, tiled=True)
-    value_piece = lax.all_gather(values_all, "ctx", axis=0, tiled=True)
+    value_piece = jnp.concatenate(
+        jax.lax.all_to_all(jnp.stack([values_all] * jax.lax.axis_size("ctx")), "ctx", 0, 0), axis=0
+    )
     block_count = key_piece.shape[0] // BLOCK
     group_size = block_group()
     others = positions

time: 1300 us -> 1330 us (1.023)
  waiting for transfers between devices: 184 us -> 227 us
  local copies, waits for them, and re-layouts: 168 us -> 140 us
  other arithmetic: 111 us -> 129 us
    all_gather x1 -> x0, waiting for transfers between devices: 119 us -> none  [body(): value_piece = lax.all_gather(values_all, 'ctx', axis=0, tiled=True)]
    all_to_all x0 -> x1, waiting for transfers between devices: none -> 83.4 us  [body(): jax.lax.all_to_all(jnp.stack([values_all] * jax.lax.axis_size('ctx')), 'c...]
    all_gather x1, waiting for transfers between devices: 7.69 us -> 82.5 us  [body(): key_piece = lax.all_gather(keys_all, 'ctx', axis=0, tiled=True)]
    reshape x1 -> x0, local copies, waits for them, and re-layouts: 22.2 us -> none  [body(): value_piece.reshape(block_count // group_size, group_size, BLOCK, HEADS,...]
    unnamed x156 -> x157, local copies, waits for them, and re-layouts: 63.5 us -> 44.1 us
    another operation x0 -> x2, local copies, waits for them, and re-layouts: none -> 17 us  [the longest x1 13 us: body(): value_piece.reshape(block_count // group_size, group_size, BLOCK, HEADS,...]
  transfers between devices with their start and end apart: 16 -> 16, of which waited for: 7 -> 7; matrix products, arithmetic and copies ran while one was open for 44% -> 43% of each run, Pallas kernels for 0% -> 0%
where the time goes in v1:
time: 1330 us
  blocking collectives  496 us (37%)
  matrix products  312 us (23%)
  waiting for transfers between devices  227 us (17%)
  local copies, waits for them, and re-layouts  140 us (11%)
  other arithmetic  129 us (10%)
  between operations  15.6 us (1%)
    psum x1, blocking collectives, body(): lax.psum((shards[0], shards[1], shards[2], shards[3], shards[4], shards[5...  430 us
    all_to_all x1, waiting for transfers between devices, body(): jax.lax.all_to_all(jnp.stack([values_all] * jax.lax.axis_size('ctx')), 'c...  83.4 us
    all_gather x1, waiting for transfers between devices, body(): key_piece = lax.all_gather(keys_all, 'ctx', axis=0, tiled=True)  82.5 us
    another operation x12, other arithmetic  49 us
    unnamed x157, local copies, waits for them, and re-layouts  44.1 us
    dot_general x2, matrix products, one_group(): jnp.einsum('ig,ghfv->ihfv', later_mask, grad_states, precision=highest)  41.2 us
    dot_general x2, matrix products, one_group(): jnp.einsum('ig,ghfv->ihfv', earlier, states, precision=highest)  38.8 us
    reduce_scatter x1, waiting for transfers between devices, body(): lax.psum_scatter(grad_value_full.astype(jnp.bfloat16), 'fsdp', scatter_di...  34.4 us
  transfers between devices with their start and end apart: 16, of which 7 were waited for; matrix products, arithmetic and copies ran while one was open for 43% of the time, Pallas kernels for 0%

profile of v1, /device:TPU:0, one launch (start us, length us, event | category | flops | bytes accessed | tf_op | source)
XLA Modules:
  0.0 1328.2 jit_solution(4195033928369212909)
XLA Ops:
  16.2 9.4 all_gather.42
  83.5 82.5 %all-gather.13.cloned.1.call-done = bf16[4096,256]{1,0:T(8,128)(2,1)} async-done(((bf16[512,256]{1,0:T(8,128)(2,1)}), bf16[4096,256]{1,0:T(8,128)(2,1)}) %all-gather.13.cloned.1.call-update) | async-done | bytes 2097168 | tf_op jit(solution)/shard_map/all_gather | solution.py:116
  173.6 83.4 %all-to-all-done = bf16[8,512,1024]{1,2,0:T(8,128)(2,1)} async-done(((bf16[8,512,1024]{1,2,0:T(8,128)(2,1)}), bf16[8,512,1024]{1,2,0:T(8,128)(2,1)}, u32[]{:S(2)}, u32[]{:S(2)}) %all-to-all-start) | async-done | bytes 8388640 | tf_op jit(solution)/shard_map/all_to_all | solution.py:118
  257.0 11.6 copy.111
  268.6 13.0 reshape_reshape.3
  281.6 122.0 %while.26 = (s32[]{:T(128)}, f32[2,16,273,64]{2,0,3,1:T(2,128)S(1)}, f32[2,16,273]{2,0,1:T(2,128)S(1)}, s32[2,8]{1,0:T(2,128)S(1)}, s32[2]{0:T(128)S(1)}, /*inde...) while((s32[]{:T(128)}, ...), condition=%wide.region_3.4_spmd.clone, body=%wide.region_1.3_spmd.clone.sunk | while | flops 1343690752 | bytes 125476048 | solution.py:143
  284.4 8.8 multiply_convert_fusion.11
  295.7 15.8 %fusion.179 = f32[8,16,273,64]{2,3,1,0:T(8,128)} fusion(bf16[8,256,16,256]{1,3,2,0:T(8,128)(2,1)} %bitcast.288, bf16[8,256,16,16]{1,3,2,0:T(8,128)(2,1)} %get-tuple-element.357, bf16[273]{0:T(512)(128)(2,1)S(1)} %pad.clone.2, bf16[1,8,256,16,64]{2,1,0,4,3:T(8,128)(2,1)} %constant_dynamic-slice_fusion.11), kind=kOutput, calls=%fused_computation.5.clone.1 | convolution fusion | flops 1198718976 | bytes 30966306 | tf_op jit(solution)/shard_map/while/body/eval_jaxpr/gthf,gthv->ghfv/dot_general | solution.py:130
  311.5 19.4 %select_add_fusion.4 = f32[2,16,273,64]{2,0,3,1:T(2,128)S(1)} fusion(f32[2,16,273,64]{2,0,3,1:T(2,128)S(1)} %get-tuple-element.380, pred[]{:T(512)S(6)} %compare.6, f32[8,16,273,64]{2,3,1,0:T(8,128)} %fusion.179, s32[8]{0:T(128)S(1)} %fusion.180, s32[2]{0:T(128)S(1)} %get-tuple-element.394), kind=kOutput, calls=%fused_computation.8.clone.1 | convolution fusion | flops 54792208 | bytes 13418537 | tf_op jit(solution)/shard_map/while/body/eval_jaxpr/ig,ghfv->ihfv/dot_general | solution.py:137
  330.9 11.8 convert_reduce_fusion.2
  345.8 8.8 multiply_convert_fusion.11
  357.0 14.6 %fusion.179 = f32[8,16,273,64]{2,3,1,0:T(8,128)} fusion(bf16[8,256,16,256]{1,3,2,0:T(8,128)(2,1)} %bitcast.288, bf16[8,256,16,16]{1,3,2,0:T(8,128)(2,1)} %get-tuple-element.357, bf16[273]{0:T(512)(128)(2,1)S(1)} %pad.clone.2, bf16[1,8,256,16,64]{2,1,0,4,3:T(8,128)(2,1)} %constant_dynamic-slice_fusion.11), kind=kOutput, calls=%fused_computation.5.clone.1 | convolution fusion | flops 1198718976 | bytes 30966306 | tf_op jit(solution)/shard_map/while/body/eval_jaxpr/gthf,gthv->ghfv/dot_general | solution.py:130
  371.6 19.4 %select_add_fusion.4 = f32[2,16,273,64]{2,0,3,1:T(2,128)S(1)} fusion(f32[2,16,273,64]{2,0,3,1:T(2,128)S(1)} %get-tuple-element.380, pred[]{:T(512)S(6)} %compare.6, f32[8,16,273,64]{2,3,1,0:T(8,128)} %fusion.179, s32[8]{0:T(128)S(1)} %fusion.180, s32[2]{0:T(128)S(1)} %get-tuple-element.394), kind=kOutput, calls=%fused_computation.8.clone.1 | convolution fusion | flops 54792208 | bytes 13418537 | tf_op jit(solution)/shard_map/while/body/eval_jaxpr/ig,ghfv->ihfv/dot_general | solution.py:137
  391.0 11.8 convert_reduce_fusion.2
  433.2 8.5 fusion.122
  441.7 12.3 multiply_convert_fusion.5
  504.9 16.4 %fusion.41 = f32[2,256,16,16]{1,3,2,0:T(8,128)S(1)} fusion(f32[2,256,16,16,16]{1,4,3,2,0:T(8,128)} %bitcast.296, f32[2,256,16,16]{1,3,2,0:T(8,128)S(1)} %copy-done.21), kind=kLoop, calls=%fused_computation.66 | loop fusion | flops 6160384 | bytes 9437184 | tf_op jit(solution)/shard_map/...ab,...b->...a/dot_general | solution.py:30
  565.0 31.4 %all_gather.51 = bf16[4096,16]{0,1:T(8,128)(2,1)S(1)} all-gather(bf16[512,16]{0,1:T(8,128)(2,1)S(1)} %bitcast.325), channel_id=1, replica_groups=mesh['ctx'=8,'fsdp'=4] {'ctx'}, dimensions={0}, use_global_device_ids=true | all-gather | bytes 147456 | tf_op jit(solution)/shard_map/all_gather | solution.py:220
  605.5 22.2 %reshape.268 = bf16[2,8,256,16,64]{4,3,2,1,0:T(8,128)(2,1)} reshape(bf16[4096,1024]{1,0:T(8,128)(2,1)} %all-gather.25.cloned.1.call-done) | data formatting | bytes 16777216 | tf_op jit(solution)/shard_map/reshape | solution.py:225
  627.7 19.7 %copy.136 = bf16[2,8,256,16,64]{2,4,3,1,0:T(8,128)(2,1)} copy(bf16[2,8,256,16,64]{4,3,2,1,0:T(8,128)(2,1)} %reshape.268) | data formatting | bytes 16777216
  647.4 111.1 %while.27 = (s32[]{:T(128)}, f32[2,16,273,64]{2,0,3,1:T(2,128)S(1)}, f32[2,16,273]{2,0,1:T(2,128)S(1)}, s32[2,8]{1,0:T(2,128)S(1)}, s32[2]{0:T(128)S(1)}, /*inde...) while((s32[]{:T(128)}, ...), condition=%wide.region_9.10_spmd.clone, body=%wide.region_8.9_spmd.clone.sunk | while | flops 1352671360 | bytes 92249264 | solution.py:248
  650.2 8.7 multiply_convert_fusion.12
  659.0 13.5 %fusion.186 = f32[8,16,273,64]{2,3,1,0:T(8,128)} fusion(bf16[8,256,16,256]{1,3,2,0:T(8,128)(2,1)} %bitcast.290, bf16[8,256,16,16]{1,3,2,0:T(8,128)(2,1)} %get-tuple-element.367, bf16[273]{0:T(512)(128)(2,1)S(1)} %pad.3.clone.2, bf16[2,8,256,16,64]{2,4,3,1,0:T(8,128)(2,1)} %get-tuple-element.431, s32[]{:T(128)S(6)} %copy.291), kind=kOutput, calls=%fused_computation.29.clone.1 | convolution fusion | flops 1198718976 | bytes 30966310 | tf_op jit(solution)/shard_map/while/body/eval_jaxpr/gthf,gthv->ghfv/dot_general | solution.py:232
  672.4 20.5 %select_add_fusion.5 = f32[2,16,273,64]{2,0,3,1:T(2,128)S(1)} fusion(f32[2,16,273,64]{2,0,3,1:T(2,128)S(1)} %get-tuple-element.414, pred[]{:T(512)S(6)} %compare.7, f32[8,16,273,64]{2,3,1,0:T(8,128)} %fusion.186, s32[8]{0:T(128)S(1)} %fusion.187, s32[2]{0:T(128)S(1)} %get-tuple-element.429), kind=kOutput, calls=%fused_computation.34.clone.1 | convolution fusion | flops 54792208 | bytes 13418537 | tf_op jit(solution)/shard_map/while/body/eval_jaxpr/ig,ghfv->ihfv/dot_general | solution.py:242
  693.0 9.3 fusion.188
  705.4 8.7 multiply_convert_fusion.12
  714.1 13.7 %fusion.186 = f32[8,16,273,64]{2,3,1,0:T(8,128)} fusion(bf16[8,256,16,256]{1,3,2,0:T(8,128)(2,1)} %bitcast.290, bf16[8,256,16,16]{1,3,2,0:T(8,128)(2,1)} %get-tuple-element.367, bf16[273]{0:T(512)(128)(2,1)S(1)} %pad.3.clone.2, bf16[2,8,256,16,64]{2,4,3,1,0:T(8,128)(2,1)} %get-tuple-element.431, s32[]{:T(128)S(6)} %copy.291), kind=kOutput, calls=%fused_computation.29.clone.1 | convolution fusion | flops 1198718976 | bytes 30966310 | tf_op jit(solution)/shard_map/while/body/eval_jaxpr/gthf,gthv->ghfv/dot_general | solution.py:232
  727.8 20.7 %select_add_fusion.5 = f32[2,16,273,64]{2,0,3,1:T(2,128)S(1)} fusion(f32[2,16,273,64]{2,0,3,1:T(2,128)S(1)} %get-tuple-element.414, pred[]{:T(512)S(6)} %compare.7, f32[8,16,273,64]{2,3,1,0:T(8,128)} %fusion.186, s32[8]{0:T(128)S(1)} %fusion.187, s32[2]{0:T(128)S(1)} %get-tuple-element.429), kind=kOutput, calls=%fused_computation.34.clone.1 | convolution fusion | flops 54792208 | bytes 13418537 | tf_op jit(solution)/shard_map/while/body/eval_jaxpr/ig,ghfv->ihfv/dot_general | solution.py:242
  748.5 9.2 fusion.188
  771.5 17.3 %fusion.38 = f32[2,256,16,16]{1,3,2,0:T(8,128)} fusion(f32[2,256,16,16,16]{1,4,3,2,0:T(8,128)} %bitcast.297, f32[2,256,16,16]{1,3,2,0:T(8,128)S(1)} %copy-done.23), kind=kLoop, calls=%fused_computation.62 | loop fusion | flops 6160384 | bytes 9437184 | tf_op jit(solution)/shard_map/...ab,...b->...a/dot_general | solution.py:30
  856.6 34.4 %reduce-scatter.12.cloned.1.call-done = bf16[256,1024]{1,0:T(8,128)(2,1)} async-done(((bf16[1024,1024]{1,0:T(8,128)(2,1)}), bf16[256,1024]{1,0:T(8,128)(2,1)}) %reduce-scatter.12.cloned.1.call-update) | async-done | bytes 524304 | tf_op jit(solution)/shard_map/reduce_scatter | solution.py:302
  891.0 430.5 %all-reduce.5 = (f32[256]{0:T(256)}, f32[256,256]{1,0:T(8,128)}, f32[256,256]{1,0:T(8,128)}, f32[256,1024]{1,0:T(8,128)}, f32[256,1024]{1,0:T(8,128)}, /*index=5...) all-reduce(f32[256]{0:T(256)S(1)} %get-tuple-element.267, ...), channel_id=1, replica_groups=mesh['ctx'=8,'fsdp'=4] {'ctx'}, use_global_device_ids=true, to_apply=%region_13.14 | all-reduce | flops 2769408 | bytes 16617472 | tf_op jit(solution)/shard_map/psum | solution.py:321
  (328 shorter events, 303.9 us)
Async XLA Ops:
  7.2 28.8 %all-gather.11.cloned.1.call-start = ((), (), s32[]{:S(2)}) async-start(), calls=%async_computation.8 | async-start | bytes 2621440 | tf_op jit(solution)/shard_map/all_gather | solution.py:71
  7.9 28.1 %copy-start.10 = (bf16[1,512,1024]{2,1,0:T(8,128)(2,1)S(1)}, bf16[1,512,1024]{2,1,0:T(8,128)(2,1)}, u32[]{:S(2)}) copy-start(bf16[1,512,1024]{2,1,0:T(8,128)(2,1)} %param.16) | copy-start | bytes 3145732
  7.9 158.1 %all-gather.13.cloned.1.call-start = ((), (), s32[]{:S(2)}) async-start(), calls=%async_computation.9 | async-start | bytes 2359296 | tf_op jit(solution)/shard_map/all_gather | solution.py:116
  14.7 42.7 %copy-start.53 = (f32[4,1,256]{2,1,0:T(1,128)}, f32[4,1,256]{2,1,0:T(1,128)S(1)}, u32[]{:S(2)}) copy-start(f32[4,1,256]{2,1,0:T(1,128)S(1)} %convert_element_type.281) | copy-start | bytes 12292
  26.3 31.2 %copy-start.58 = (f32[512]{0:T(512)}, f32[512]{0:T(512)S(1)}, u32[]{:S(2)}) copy-start(f32[512]{0:T(512)S(1)} %get-tuple-element.253) | copy-start | bytes 6148
  28.9 389.7 %all-gather.15.cloned.1.call-start = ((), (), s32[]{:S(2)}) async-start(), calls=%async_computation.10 | async-start | bytes 2621440 | tf_op jit(solution)/shard_map/all_gather | solution.py:72
  29.6 395.0 %all-gather.17.cloned.1.call-start = ((), (), s32[]{:S(2)}) async-start(), calls=%async_computation.11 | async-start | bytes 7045120 | tf_op jit(solution)/shard_map/all_gather | solution.py:74
  30.2 402.9 %all-gather.19.cloned.1.call-start = ((), (), s32[]{:S(2)}) async-start(), calls=%async_computation.12 | async-start | bytes 7045120 | tf_op jit(solution)/shard_map/all_gather | solution.py:75
  43.5 213.5 %all-to-all-start = ((bf16[8,512,1024]{1,2,0:T(8,128)(2,1)}), bf16[8,512,1024]{1,2,0:T(8,128)(2,1)}, u32[]{:S(2)}, u32[]{:S(2)}) async-start(bf16[8,512,1024]{1,2,0:T(8,128)(2,1)} %stack.2), calls=%async_computation | async-start | bytes 16777216 | tf_op jit(solution)/shard_map/all_to_all | solution.py:118
  49.6 392.1 %all-gather.21.cloned.1.call-start = ((), (), s32[]{:S(2)}) async-start(), calls=%async_computation.13 | async-start | bytes 7045120 | tf_op jit(solution)/shard_map/all_gather | solution.py:76
  50.2 507.1 %all-gather.23.cloned.1.call-start = ((), (), s32[]{:S(2)}) async-start(), calls=%async_computation.14 | async-start | bytes 2359296 | tf_op jit(solution)/shard_map/all_gather | solution.py:218
  59.4 546.1 %all-gather.25.cloned.1.call-start = ((), (), s32[]{:S(2)}) async-start(), calls=%async_computation.15 | async-start | bytes 9437184 | tf_op jit(solution)/shard_map/all_gather | solution.py:219
  63.2 18.1 %copy-start.28 = (bf16[2,256,16,16]{1,0,3,2:T(2,128)(2,1)}, bf16[2,256,16,16]{1,0,3,2:T(2,128)(2,1)S(1)}, u32[]{:S(2)}) copy-start(bf16[2,256,16,16]{1,0,3,2:T(2,128)(2,1)S(1)} %reshape.240) | copy-start | bytes 786436
  281.6 122.0 %copy-start.44 = (bf16[2,256,16,16]{1,3,2,0:T(8,128)(2,1)S(1)}, bf16[2,256,16,16]{1,3,2,0:T(8,128)(2,1)}, u32[]{:S(2)}) copy-start(bf16[2,256,16,16]{1,3,2,0:T(8,128)(2,1)} %get-tuple-element.250) | copy-start | bytes 786436
  281.6 122.0 %copy-start.64 = (bf16[273]{0:T(512)(128)(2,1)S(1)}, bf16[273]{0:T(512)(128)(2,1)}, u32[]{:S(2)}) copy-start(bf16[273]{0:T(512)(128)(2,1)} %pad.9.clone) | copy-start | bytes 1642
  311.5 19.4 %copy-start = (bf16[8,256,16,16]{1,3,2,0:T(8,128)(2,1)S(1)}, bf16[8,256,16,16]{1,3,2,0:T(8,128)(2,1)}, u32[]{:S(2)}) copy-start(bf16[8,256,16,16]{1,3,2,0:T(8,128)(2,1)} %get-tuple-element.357) | copy-start | bytes 3145732 | tf_op jit(solution)/shard_map/while
  371.6 19.4 %copy-start = (bf16[8,256,16,16]{1,3,2,0:T(8,128)(2,1)S(1)}, bf16[8,256,16,16]{1,3,2,0:T(8,128)(2,1)}, u32[]{:S(2)}) copy-start(bf16[8,256,16,16]{1,3,2,0:T(8,128)(2,1)} %get-tuple-element.357) | copy-start | bytes 3145732 | tf_op jit(solution)/shard_map/while
  479.4 345.5 %reduce-scatter.8.cloned.1.call-start = ((), (), s32[]{:S(2)}) async-start(), calls=%async_computation.16 | async-start | bytes 655360 | tf_op jit(solution)/shard_map/reduce_scatter | solution.py:296
  491.6 29.7 %copy-start.9 = (bf16[2,256,16,64]{1,3,2,0:T(8,128)(2,1)}, bf16[2,256,16,64]{1,3,2,0:T(8,128)(2,1)S(1)}, u32[]{:S(2)}) copy-start(bf16[2,256,16,64]{1,3,2,0:T(8,128)(2,1)S(1)} %get-tuple-element.246) | copy-start | bytes 3145732
  533.8 291.2 %reduce-scatter.14.cloned.1.call-start = ((), (), s32[]{:S(2)}) async-start(), calls=%async_computation.19 | async-start | bytes 2621440 | tf_op jit(solution)/shard_map/reduce_scatter | solution.py:305
  536.5 288.5 %reduce-scatter.16.cloned.1.call-start = ((), (), s32[]{:S(2)}) async-start(), calls=%async_computation.20 | async-start | bytes 7045120 | tf_op jit(solution)/shard_map/reduce_scatter | solution.py:311
  544.2 280.8 %reduce-scatter.18.cloned.1.call-start = ((), (), s32[]{:S(2)}) async-start(), calls=%async_computation.21 | async-start | bytes 7045120 | tf_op jit(solution)/shard_map/reduce_scatter | solution.py:314
  552.2 279.6 %reduce-scatter.20.cloned.1.call-start = ((), (), s32[]{:S(2)}) async-start(), calls=%async_computation.22 | async-start | bytes 7045120 | tf_op jit(solution)/shard_map/reduce_scatter | solution.py:317
  561.3 35.1 %copy-start.37 = (bf16[1,512,1024]{2,1,0:T(8,128)(2,1)S(1)}, bf16[1,512,1024]{2,1,0:T(8,128)(2,1)}, u32[]{:S(2)}) copy-start(bf16[1,512,1024]{2,1,0:T(8,128)(2,1)} %param.27) | copy-start | bytes 3145732
  561.3 35.1 %copy-start.71 = (bf16[512,2752]{0,1:T(8,128)(2,1)S(1)}, bf16[512,2752]{0,1:T(8,128)(2,1)}, u32[]{:S(2)}) copy-start(bf16[512,2752]{0,1:T(8,128)(2,1)} %get-tuple-element.245) | copy-start | bytes 8454148
  601.4 255.2 %reduce-scatter.10.cloned.1.call-start = ((), (), s32[]{:S(2)}) async-start(), calls=%async_computation.17 | async-start | bytes 655360 | tf_op jit(solution)/shard_map/reduce_scatter | solution.py:299
  627.7 19.7 %copy-start.46 = (s32[2]{0:T(128)S(1)}, s32[2]{0:T(128)}, u32[]{:S(2)}) copy-start(s32[2]{0:T(128)} %copy-done.45) | copy-start | bytes 28
  627.7 19.7 %copy-start.69 = (s32[2,8]{1,0:T(2,128)S(1)}, s32[2,8]{1,0:T(2,128)}, u32[]{:S(2)}) copy-start(s32[2,8]{1,0:T(2,128)} %copy-done.68) | copy-start | bytes 196
  672.4 20.6 %copy-start.8 = (bf16[8,256,16,16]{1,3,2,0:T(8,128)(2,1)S(1)}, bf16[8,256,16,16]{1,3,2,0:T(8,128)(2,1)}, u32[]{:S(2)}) copy-start(bf16[8,256,16,16]{1,3,2,0:T(8,128)(2,1)} %get-tuple-element.367) | copy-start | bytes 3145732 | tf_op jit(solution)/shard_map/while
  727.8 20.8 %copy-start.8 = (bf16[8,256,16,16]{1,3,2,0:T(8,128)(2,1)S(1)}, bf16[8,256,16,16]{1,3,2,0:T(8,128)(2,1)}, u32[]{:S(2)}) copy-start(bf16[8,256,16,16]{1,3,2,0:T(8,128)(2,1)} %get-tuple-element.367) | copy-start | bytes 3145732 | tf_op jit(solution)/shard_map/while
  802.0 89.0 %reduce-scatter.12.cloned.1.call-start = ((), (), s32[]{:S(2)}) async-start(), calls=%async_computation.18 | async-start | bytes 2621440 | tf_op jit(solution)/shard_map/reduce_scatter | solution.py:302
  839.2 51.7 %copy-start.48 = (bf16[256,256]{1,0:T(8,128)(2,1)S(1)}, bf16[256,256]{1,0:T(8,128)(2,1)}, u32[]{:S(2)}) copy-start(bf16[256,256]{1,0:T(8,128)(2,1)} %reduce-scatter.8.cloned.1.call-done) | copy-start | bytes 393220
  (64 other events, 382.7 us)
Sparse Core Ops, SparseCore 0:
  9.6 26.3 all-gather.10
  38.7 127.2 all-gather.12
  167.6 32.2 all-gather.14
  201.3 43.3 all-gather.16
  246.1 43.3 all-gather.18
  291.0 42.6 all-gather.20
  335.8 49.2 all-gather.22
  479.6 125.8 all-gather.24
  608.0 19.9 reduce-scatter.7
  630.5 31.4 reduce-scatter.13
  664.5 53.9 reduce-scatter.15
  721.2 54.0 reduce-scatter.17
  777.8 54.0 reduce-scatter.19
  834.9 21.6 reduce-scatter.9
  859.5 31.4 reduce-scatter.11
